TPU v7x, 256 devices: a whole 4x4x8 slice. The times are simulated.
256 devices in a mesh: dp: 8 (over x, core), tm: 32 (over z, y).
Axes of the slice: x: 4, y: 4, z: 8, core: 2. Of those that a mesh axis runs over, the one named last changes fastest.
Arguments:
- latents: bfloat16 [8, 17, 64, 64, 256], P('dp', None, 'tm'), may hold values from -6 to 6
- cotangent: bfloat16 [8, 17, 64, 64, 256], P('dp', None, 'tm'), may hold values from -6 to 6
- spatial_weight: bfloat16 [3, 3, 256, 256], replicated, may hold values from -0.125 to 0.125
- temporal_weight: bfloat16 [3, 256, 256], replicated, may hold values from -0.21875 to 0.21875
Outputs:
- block_out: bfloat16 [8, 17, 64, 64, 256], P('dp', None, 'tm')
- latents_grad: bfloat16 [8, 17, 64, 64, 256], P('dp', None, 'tm')
- spatial_grad: float32 [3, 3, 256, 256], replicated
- temporal_grad: float32 [3, 256, 256], replicated
All inputs are finite; a program needn't handle non-finite values.
Results may differ from a plain program's by a relative error of at most 0.0085.
Values may be sent and summed in bfloat16 or wider, within the bound.
A program may use at most 64 MiB of HBM per device.

v0:
```python
import jax
import jax.numpy as jnp
from jax import lax
from jax.sharding import PartitionSpec as P


def with_halo(cells, sides, width):
    for axis, dim in sides:
        count = lax.axis_size(axis)
        ends = count - 1
        head = lax.slice_in_dim(cells, 0, width, axis=dim)
        tail = lax.slice_in_dim(cells, cells.shape[dim] - width, cells.shape[dim], axis=dim)
        cells = jnp.concatenate(
            [
                lax.ppermute(tail, axis, [(i, (i + 1) % count) for i in range(ends)]),
                cells,
                lax.ppermute(head, axis, [((i + 1) % count, i) for i in range(ends)]),
            ],
            axis=dim,
        )
    return cells


def band_patches(extended, rows_out, flipped):
    padded = jnp.pad(extended, ((0, 0), (0, 0), (1, 1), (0, 0)))
    cols = extended.shape[2]
    pieces = []
    for first in range(3):
        for second in range(3):
            top = 2 - first if flipped else first
            left = 2 - second if flipped else second
            pieces.append(padded[:, top : top + rows_out, left : left + cols, :])
    return jnp.concatenate(pieces, axis=3).reshape(-1, 9 * extended.shape[3])


def causal_mix(act, weight):
    clips, frames, cells, chans = act.shape
    padded = jnp.pad(act, ((0, 0), (2, 0), (0, 0), (0, 0)))
    total = jnp.zeros((clips * frames * cells, chans), jnp.float32)
    for tap in range(3):
        earlier = padded[:, 2 - tap : 2 - tap + frames].reshape(-1, chans)
        total = total + jnp.dot(earlier, weight[tap], preferred_element_type=jnp.float32)
    return total.astype(jnp.bfloat16)


def anti_mix(cot, weight):
    clips, frames, cells, chans = cot.shape
    padded = jnp.pad(cot, ((0, 0), (0, 2), (0, 0), (0, 0)))
    total = jnp.zeros((clips * frames * cells, chans), jnp.float32)
    for tap in range(3):
        later = padded[:, tap : tap + frames].reshape(-1, chans)
        total = total + lax.dot_general(
            later, weight[tap], (((1,), (1,)), ((), ())), preferred_element_type=jnp.float32
        )
    return total.astype(jnp.bfloat16)


def tap_grads(act, cot):
    clips, frames, cells, chans = act.shape
    padded = jnp.pad(act, ((0, 0), (2, 0), (0, 0), (0, 0)))
    cot_flat = cot.reshape(-1, chans)
    parts = []
    for tap in range(3):
        earlier = padded[:, 2 - tap : 2 - tap + frames].reshape(-1, chans)
        parts.append(
            lax.dot_general(
                earlier, cot_flat, (((0,), (0,)), ((), ())), preferred_element_type=jnp.float32
            )
        )
    return jnp.stack(parts)


def silu_grad(act_grad, pre):
    sig = jax.nn.sigmoid(pre)
    return (act_grad.astype(jnp.float32) * sig * (1.0 + pre * (1.0 - sig))).astype(jnp.bfloat16)


def body(latents, cotangent, spatial_weight, temporal_weight):
    clips, frames, rows, cols, chans = latents.shape
    flat_w = spatial_weight.reshape(9 * chans, chans)
    flip_w = jnp.transpose(spatial_weight, (0, 1, 3, 2)).reshape(9 * chans, chans)
    cot_band = cotangent.reshape(clips, frames, rows * cols, chans)
    extended = with_halo(latents, (("tm", 2),), 1)
    patches = band_patches(extended.reshape(clips * frames, rows + 2, cols, chans), rows, False)
    pre = jnp.dot(patches, flat_w, preferred_element_type=jnp.float32)
    act = jax.nn.silu(pre).astype(jnp.bfloat16).reshape(clips, frames, rows * cols, chans)
    mixed = causal_mix(act, temporal_weight)
    act_grad = anti_mix(cot_band, temporal_weight)
    pre_grad = silu_grad(act_grad, pre)
    grad_ext = with_halo(pre_grad.reshape(clips, frames, rows, cols, chans), (("tm", 2),), 1)
    back = jnp.dot(
        band_patches(grad_ext.reshape(clips * frames, rows + 2, cols, chans), rows, True),
        flip_w,
        preferred_element_type=jnp.float32,
    )
    temporal_local = tap_grads(act, cot_band)
    block_out = (latents.reshape(-1, chans).astype(jnp.float32) + mixed.astype(jnp.float32)).astype(
        jnp.bfloat16
    )
    latents_grad = (cotangent.reshape(-1, chans).astype(jnp.float32) + back).astype(jnp.bfloat16)
    spatial_local = lax.dot_general(
        patches, pre_grad, (((0,), (0,)), ((), ())), preferred_element_type=jnp.float32
    )
    spatial_sum, temporal_sum = lax.psum((spatial_local, temporal_local), ("dp", "tm"))
    scale = (clips * lax.axis_size("dp") * frames * rows * lax.axis_size("tm") * cols) ** (-0.5)
    return (
        block_out.reshape(latents.shape),
        latents_grad.reshape(latents.shape),
        (spatial_sum * scale).reshape(3, 3, chans, chans),
        temporal_sum * scale,
    )


def solution(mesh):
    in_specs = (P("dp", None, "tm", None, None), P("dp", None, "tm", None, None), P(), P())
    out_specs = (P("dp", None, "tm", None, None), P("dp", None, "tm", None, None), P(), P())
    return jax.shard_map(body, mesh=mesh, in_specs=in_specs, out_specs=out_specs, check_vma=False)
```

profile of v0, /device:TPU:2, one launch (start us, length us, event | category | flops | bytes accessed | tf_op | source)
XLA Modules:
  0.0 338.0 jit_solution(11071545228273672446)
XLA Ops:
  7.2 2.4 fusion.37
  9.6 4.4 %collective-permute-start = (bf16[1,17,1,64,256]{4,3,2,1,0:T(8,128)(2,1)}, bf16[1,17,1,64,256]{4,3,2,1,0:T(8,128)(2,1)}, u32[]{:S(2)}, u32[]{:S(2)}) collective-permute-start(bf16[1,17,1,64,256]{4,3,2,1,0:T(8,128)(2,1)} %get-tuple-element.12), channel_id=1, source_target_pairs={{0,1},{1,2},{2,3},{3,4},{4,5},{5,6},{6,7},{7,8},{8,9},{9,10},{10,1... | collective-permute-start | bytes 1671176 | tf_op jit(solution)/shard_map/ppermute | solution.py:15
  14.1 1.3 collective-permute-start.1
  15.4 2.8 fusion.26
  18.1 1.5 copy.8
  19.9 1.4 copy-done.3
  21.8 3.6 %collective-permute-done = bf16[1,17,1,64,256]{4,3,2,1,0:T(8,128)(2,1)} collective-permute-done((bf16[1,17,1,64,256]{4,3,2,1,0:T(8,128)(2,1)}, bf16[1,17,1,64,256]{4,3,2,1,0:T(8,128)(2,1)}, u32[]{:S(2)}, u32[]{:S(2)}) %collective-permute-start) | collective-permute-done | bytes 557088 | tf_op jit(solution)/shard_map/ppermute | solution.py:15
  25.4 4.9 %collective-permute-done.1 = bf16[1,17,1,64,256]{4,3,2,1,0:T(8,128)(2,1)} collective-permute-done((bf16[1,17,1,64,256]{4,3,2,1,0:T(8,128)(2,1)}, bf16[1,17,1,64,256]{4,3,2,1,0:T(8,128)(2,1)}, u32[]{:S(2)}, u32[]{:S(2)}) %collective-permute-start.1) | collective-permute-done | bytes 557088 | tf_op jit(solution)/shard_map/ppermute | solution.py:17
  30.4 1.5 maximum_bitcast_fusion
  32.9 0.7 fusion.12
  34.3 0.7 fusion.14
  35.7 2.9 multiply_convert_fusion
  39.1 1.8 fusion.28
  41.0 1.0 fusion.9
  42.0 4.4 %fusion.38 = f32[2304,256]{1,0:T(8,128)} fusion(bf16[2176,2304]{1,0:T(8,128)(2,1)S(1)} %bitcast.83, bf16[2176,256]{1,0:T(8,128)(2,1)S(1)} %fusion.9), kind=kOutput, calls=%fused_computation.75 | convolution fusion | flops 2566914048 | bytes 13500416 | tf_op jit(solution)/shard_map/dot_general | solution.py:101
  46.4 1.2 fusion.36
  47.6 3.5 %collective-permute-start.2 = (bf16[1,17,1,64,256]{4,3,2,1,0:T(8,128)(2,1)}, bf16[1,17,1,64,256]{4,3,2,1,0:T(8,128)(2,1)}, u32[]{:S(2)}, u32[]{:S(2)}) collective-permute-start(bf16[1,17,1,64,256]{4,3,2,1,0:T(8,128)(2,1)} %get-tuple-element.6), channel_id=1, source_target_pairs={{0,1},{1,2},{2,3},{3,4},{4,5},{5,6},{6,7},{7,8},{8,9},{9,10},{10,1... | collective-permute-start | bytes 1671176 | tf_op jit(solution)/shard_map/ppermute | solution.py:15
  51.2 1.3 collective-permute-start.3
  53.6 0.9 pad_maximum_fusion
  54.6 2.5 convolution_add_fusion.3
  57.1 2.5 fusion.4
  59.6 1.8 collective-permute-done.2
  61.4 4.9 %collective-permute-done.3 = bf16[1,17,1,64,256]{4,3,2,1,0:T(8,128)(2,1)} collective-permute-done((bf16[1,17,1,64,256]{4,3,2,1,0:T(8,128)(2,1)}, bf16[1,17,1,64,256]{4,3,2,1,0:T(8,128)(2,1)}, u32[]{:S(2)}, u32[]{:S(2)}) %collective-permute-start.3) | collective-permute-done | bytes 557088 | tf_op jit(solution)/shard_map/ppermute | solution.py:17
  66.3 1.5 maximum_bitcast_fusion.1
  68.3 0.7 fusion.17
  69.0 0.6 fusion.18
  69.7 0.7 fusion.19
  71.1 0.7 fusion.21
  72.3 3.8 %fusion = bf16[2176,256]{1,0:T(8,128)(2,1)} fusion(bf16[2176,2304]{1,0:T(8,128)(2,1)S(1)} %bitcast.84, bf16[2304,256]{1,0:T(8,128)(2,1)S(1)} %bitcast.79, bf16[2176,256]{1,0:T(8,128)(2,1)S(1)} %bitcast.67), kind=kOutput, calls=%fused_computation.5 | convolution fusion | flops 2568585216 | bytes 13434880 | tf_op jit(solution)/shard_map/dot_general | solution.py:91
  76.1 250.7 %all-reduce.7.cloned.1.call-done = (f32[2304,256]{1,0:T(8,128)}, f32[3,256,256]{2,1,0:T(8,128)}) async-done(((f32[2304,256]{1,0:T(8,128)}, f32[3,256,256]{2,1,0:T(8,128)}), (f32[2304,256]{1,0:T(8,128)}, f32[3,256,256]{2,1,0:T(8,128)})) %all-reduce.7.cloned.1.call-update) | async-done | bytes 3145744 | tf_op jit(solution)/shard_map/psum | solution.py:104
  326.8 3.3 broadcast_multiply_fusion
  330.2 0.9 broadcast_multiply_fusion.1
  (39 shorter events, 6.7 us)
Async XLA Ops:
  7.2 8.2 %copy-start = (bf16[1,17,2,64,256]{4,3,2,1,0:T(8,128)(2,1)S(1)}, bf16[1,17,2,64,256]{4,3,2,1,0:T(8,128)(2,1)}, u32[]{:S(2)}) copy-start(bf16[1,17,2,64,256]{4,3,2,1,0:T(8,128)(2,1)} %param.5) | copy-start | bytes 3342340
  7.2 319.6 %all-reduce.7.cloned.1.call-start = ((), (), s32[]{:S(2)}) async-start(), calls=%async_computation | async-start | bytes 6291456 | tf_op jit(solution)/shard_map/psum | solution.py:104
  9.6 8.5 %copy-start.6 = (bf16[3,3,256,256]{3,2,1,0:T(8,128)(2,1)S(1)}, bf16[3,3,256,256]{3,2,1,0:T(8,128)(2,1)}, u32[]{:S(2)}) copy-start(bf16[3,3,256,256]{3,2,1,0:T(8,128)(2,1)} %param.6) | copy-start | bytes 3538948
  9.6 15.8 %collective-permute-start = (bf16[1,17,1,64,256]{4,3,2,1,0:T(8,128)(2,1)}, bf16[1,17,1,64,256]{4,3,2,1,0:T(8,128)(2,1)}, u32[]{:S(2)}, u32[]{:S(2)}) collective-permute-start(bf16[1,17,1,64,256]{4,3,2,1,0:T(8,128)(2,1)} %get-tuple-element.12), channel_id=1, source_target_pairs={{0,1},{1,2},{2,3},{3,4},{4,5},{5,6},{6,7},{7,8},{8,9},{9,10},{10,1... | collective-permute-start | bytes 1671176 | tf_op jit(solution)/shard_map/ppermute | solution.py:15
  14.1 16.3 %collective-permute-start.1 = (bf16[1,17,1,64,256]{4,3,2,1,0:T(8,128)(2,1)}, bf16[1,17,1,64,256]{4,3,2,1,0:T(8,128)(2,1)}, u32[]{:S(2)}, u32[]{:S(2)}) collective-permute-start(bf16[1,17,1,64,256]{4,3,2,1,0:T(8,128)(2,1)} %get-tuple-element.13), channel_id=1, source_target_pairs={{1,0},{2,1},{3,2},{4,3},{5,4},{6,5},{7,6},{8,7},{9,8},{10,9},{11,1... | collective-permute-start | bytes 1671176 | tf_op jit(solution)/shard_map/ppermute | solution.py:17
  19.7 1.6 copy-start.3
  19.7 1.7 copy-start.8
  21.3 9.0 %copy-start.1 = (bf16[1,17,2,64,256]{4,3,2,1,0:T(8,128)(2,1)S(1)}, bf16[1,17,2,64,256]{4,3,2,1,0:T(8,128)(2,1)}, u32[]{:S(2)}) copy-start(bf16[1,17,2,64,256]{4,3,2,1,0:T(8,128)(2,1)} %param.4) | copy-start | bytes 3342340
  42.0 4.4 %copy-start.4 = (bf16[2176,256]{1,0:T(8,128)(2,1)}, bf16[2176,256]{1,0:T(8,128)(2,1)S(1)}, u32[]{:S(2)}) copy-start(bf16[2176,256]{1,0:T(8,128)(2,1)S(1)} %fusion.9) | copy-start | bytes 3342340
  47.6 13.7 %collective-permute-start.2 = (bf16[1,17,1,64,256]{4,3,2,1,0:T(8,128)(2,1)}, bf16[1,17,1,64,256]{4,3,2,1,0:T(8,128)(2,1)}, u32[]{:S(2)}, u32[]{:S(2)}) collective-permute-start(bf16[1,17,1,64,256]{4,3,2,1,0:T(8,128)(2,1)} %get-tuple-element.6), channel_id=1, source_target_pairs={{0,1},{1,2},{2,3},{3,4},{4,5},{5,6},{6,7},{7,8},{8,9},{9,10},{10,1... | collective-permute-start | bytes 1671176 | tf_op jit(solution)/shard_map/ppermute | solution.py:15
  51.2 15.1 %collective-permute-start.3 = (bf16[1,17,1,64,256]{4,3,2,1,0:T(8,128)(2,1)}, bf16[1,17,1,64,256]{4,3,2,1,0:T(8,128)(2,1)}, u32[]{:S(2)}, u32[]{:S(2)}) collective-permute-start(bf16[1,17,1,64,256]{4,3,2,1,0:T(8,128)(2,1)} %get-tuple-element.7), channel_id=1, source_target_pairs={{1,0},{2,1},{3,2},{4,3},{5,4},{6,5},{7,6},{8,7},{9,8},{10,9},{11,1... | collective-permute-start | bytes 1671176 | tf_op jit(solution)/shard_map/ppermute | solution.py:17
  52.6 1.0 copy-start.2
  57.1 9.2 %copy-start.5 = (bf16[2176,256]{1,0:T(8,128)(2,1)S(1)}, bf16[2176,256]{1,0:T(8,128)(2,1)}, u32[]{:S(2)}) copy-start(bf16[2176,256]{1,0:T(8,128)(2,1)} %copy-done.4) | copy-start | bytes 3342340
  71.0 1.3 copy-start.7
  326.8 3.4 copy-start.9
Sparse Core Ops, SparseCore 0:
  54.7 272.0 all-reduce.6
where the time goes:
time: 338 us
  waiting for transfers between devices  266 us (79%)
  matrix products  23.6 us (7%)
  local copies, waits for them, and re-layouts  15.4 us (5%)
  between operations  14.3 us (4%)
  starting transfers between devices  10.5 us (3%)
  other arithmetic  8.16 us (2%)
    psum x1, waiting for transfers between devices, body(): lax.psum((spatial_local, temporal_local), ('dp', 'tm'))  251 us
    unnamed x37, local copies, waits for them, and re-layouts  10.1 us
    ppermute x2, waiting for transfers between devices, with_halo(): lax.ppermute(head, axis, [((i + 1) % count, i) for i in range(ends)])  9.86 us
    ppermute x2, starting transfers between devices, with_halo(): lax.ppermute(tail, axis, [(i, (i + 1) % count) for i in range(ends)])  7.93 us
    dot_general x3, matrix products, causal_mix(): jnp.dot(earlier, weight[tap], preferred_element_type=jnp.float32)  6.79 us
  transfers between devices with their start and end apart: 5, of which 5 were waited for; matrix products, arithmetic and copies ran while one was open for 6% of the time, Pallas kernels for 0%

commit v1 on v0

--- a/solution.py
+++ b/solution.py
@@ -101,7 +101,7 @@
     spatial_local = lax.dot_general(
         patches, pre_grad, (((0,), (0,)), ((), ())), preferred_element_type=jnp.float32
     )
-    spatial_sum, temporal_sum = lax.psum((spatial_local, temporal_local), ("dp", "tm"))
+    spatial_sum, temporal_sum = lax.psum(lax.psum((spatial_local, temporal_local), "dp"), "tm")
     scale = (clips * lax.axis_size("dp") * frames * rows * lax.axis_size("tm") * cols) ** (-0.5)
     return (
         block_out.reshape(latents.shape),

time: 338 us -> 297 us (0.88)
  waiting for transfers between devices: 266 us -> 227 us
    psum x1 -> x2, waiting for transfers between devices: 251 us -> 214 us  [the longest x1 150 us: body(): lax.psum(lax.psum((spatial_local, temporal_local), 'dp'), 'tm')]
    ppermute x2, waiting for transfers between devices: 9.86 us -> 4.15 us  [with_halo(): lax.ppermute(head, axis, [((i + 1) % count, i) for i in range(ends)])]
    ppermute x2, waiting for transfers between devices: 5.39 us -> 9.35 us  [with_halo(): lax.ppermute(tail, axis, [(i, (i + 1) % count) for i in range(ends)])]
    unnamed x37 -> x39, local copies, waits for them, and re-layouts: 10.1 us -> 10.1 us
  transfers between devices with their start and end apart: 5 -> 6, of which waited for: 5 -> 4; matrix products, arithmetic and copies ran while one was open for 6% -> 8% of each run, Pallas kernels for 0% -> 0%
where the time goes in v1:
time: 297 us
  waiting for transfers between devices  227 us (76%)
  matrix products  22.3 us (8%)
  local copies, waits for them, and re-layouts  15.8 us (5%)
  between operations  14.4 us (5%)
  starting transfers between devices  10.4 us (4%)
  other arithmetic  6.95 us (2%)
    psum x1, waiting for transfers between devices, body(): lax.psum(lax.psum((spatial_local, temporal_local), 'dp'), 'tm')  150 us
    psum x1, waiting for transfers between devices, body(): lax.psum((spatial_local, temporal_local), 'dp')  63.5 us
    unnamed x39, local copies, waits for them, and re-layouts  10.1 us
    ppermute x2, waiting for transfers between devices, with_halo(): lax.ppermute(tail, axis, [(i, (i + 1) % count) for i in range(ends)])  9.35 us
    ppermute x2, starting transfers between devices, with_halo(): lax.ppermute(tail, axis, [(i, (i + 1) % count) for i in range(ends)])  7.78 us
    dot_general x3, matrix products, causal_mix(): jnp.dot(earlier, weight[tap], preferred_element_type=jnp.float32)  7.72 us
  transfers between devices with their start and end apart: 6, of which 4 were waited for; matrix products, arithmetic and copies ran while one was open for 8% of the time, Pallas kernels for 0%

profile of v1, /device:TPU:2, one launch (start us, length us, event | category | flops | bytes accessed | tf_op | source)
XLA Modules:
  0.0 297.0 jit_solution(10611479128560798154)
XLA Ops:
  7.2 1.4 fusion.37
  8.6 3.5 %collective-permute-start = (bf16[1,17,1,64,256]{4,3,2,1,0:T(8,128)(2,1)S(1)}, bf16[1,17,1,64,256]{4,3,2,1,0:T(8,128)(2,1)S(1)}, u32[]{:S(2)}, u32[]{:S(2)}) collective-permute-start(bf16[1,17,1,64,256]{4,3,2,1,0:T(8,128)(2,1)S(1)} %get-tuple-element.14), channel_id=1, source_target_pairs={{0,1},{1,2},{2,3},{3,4},{4,5},{5,6},{6,7},{7,8},{8,9},{9,10},{10,1... | collective-permute-start | bytes 1671176 | tf_op jit(solution)/shard_map/ppermute | solution.py:15
  12.2 1.3 collective-permute-start.1
  14.7 9.3 %collective-permute-done = bf16[1,17,1,64,256]{4,3,2,1,0:T(8,128)(2,1)S(1)} collective-permute-done((bf16[1,17,1,64,256]{4,3,2,1,0:T(8,128)(2,1)S(1)}, bf16[1,17,1,64,256]{4,3,2,1,0:T(8,128)(2,1)S(1)}, u32[]{:S(2)}, u32[]{:S(2)}) %collective-permute-start) | collective-permute-done | bytes 557088 | tf_op jit(solution)/shard_map/ppermute | solution.py:15
  24.0 4.1 %collective-permute-done.1 = bf16[1,17,1,64,256]{4,3,2,1,0:T(8,128)(2,1)S(1)} collective-permute-done((bf16[1,17,1,64,256]{4,3,2,1,0:T(8,128)(2,1)S(1)}, bf16[1,17,1,64,256]{4,3,2,1,0:T(8,128)(2,1)S(1)}, u32[]{:S(2)}, u32[]{:S(2)}) %collective-permute-start.1) | collective-permute-done | bytes 557088 | tf_op jit(solution)/shard_map/ppermute | solution.py:17
  29.4 0.7 fusion.12
  30.3 0.6 fusion.13
  30.9 0.7 fusion.14
  31.7 0.6 fusion.15
  32.3 0.7 copy-done.7
  32.9 2.9 multiply_convert_fusion
  35.9 1.0 fusion.9
  36.9 4.4 %fusion.38 = f32[2304,256]{1,0:T(8,128)} fusion(bf16[2176,2304]{1,0:T(8,128)(2,1)S(1)} %bitcast.83, bf16[2176,256]{1,0:T(8,128)(2,1)S(1)} %fusion.9), kind=kOutput, calls=%fused_computation.75 | convolution fusion | flops 2566914048 | bytes 13500416 | tf_op jit(solution)/shard_map/dot_general | solution.py:101
  43.2 0.9 pad_maximum_fusion
  44.2 2.4 copy.8
  46.6 2.5 fusion.36
  49.1 4.3 %collective-permute-start.2 = (bf16[1,17,1,64,256]{4,3,2,1,0:T(8,128)(2,1)}, bf16[1,17,1,64,256]{4,3,2,1,0:T(8,128)(2,1)}, u32[]{:S(2)}, u32[]{:S(2)}) collective-permute-start(bf16[1,17,1,64,256]{4,3,2,1,0:T(8,128)(2,1)} %get-tuple-element.8), channel_id=1, source_target_pairs={{0,1},{1,2},{2,3},{3,4},{4,5},{5,6},{6,7},{7,8},{8,9},{9,10},{10,1... | collective-permute-start | bytes 1671176 | tf_op jit(solution)/shard_map/ppermute | solution.py:15
  53.4 1.3 collective-permute-start.3
  54.7 2.8 fusion.28
  57.4 63.5 %all-reduce.11.cloned.1.call-done = (f32[2304,256]{1,0:T(8,128)}, f32[3,256,256]{2,1,0:T(8,128)}) async-done(((f32[2304,256]{1,0:T(8,128)}, f32[3,256,256]{2,1,0:T(8,128)}), (f32[2304,256]{1,0:T(8,128)}, f32[3,256,256]{2,1,0:T(8,128)})) %all-reduce.11.cloned.1.call-update) | async-done | bytes 3145744 | tf_op jit(solution)/shard_map/psum | solution.py:104
  120.9 2.5 convolution_add_fusion.3
  123.4 2.5 fusion.4
  125.9 1.5 maximum_bitcast_fusion.1
  127.9 0.7 fusion.17
  128.6 0.6 fusion.18
  129.3 0.7 fusion.19
  130.0 0.6 fusion.20
  130.7 0.7 fusion.21
  131.9 3.8 %fusion = bf16[2176,256]{1,0:T(8,128)(2,1)} fusion(bf16[2176,2304]{1,0:T(8,128)(2,1)S(1)} %bitcast.84, bf16[2304,256]{1,0:T(8,128)(2,1)S(1)} %bitcast.79, bf16[2176,256]{1,0:T(8,128)(2,1)S(1)} %bitcast.67), kind=kOutput, calls=%fused_computation.5 | convolution fusion | flops 2568585216 | bytes 13434880 | tf_op jit(solution)/shard_map/dot_general | solution.py:91
  135.7 150.1 %all-reduce.9.cloned.1.call-done = (f32[2304,256]{1,0:T(8,128)}, f32[3,256,256]{2,1,0:T(8,128)}) async-done(((f32[2304,256]{1,0:T(8,128)}, f32[3,256,256]{2,1,0:T(8,128)}), (f32[2304,256]{1,0:T(8,128)}, f32[3,256,256]{2,1,0:T(8,128)})) %all-reduce.9.cloned.1.call-update) | async-done | bytes 3145744 | tf_op jit(solution)/shard_map/psum | solution.py:104
  285.8 3.3 %broadcast_multiply_fusion = f32[2304,256]{1,0:T(8,128)} fusion(f32[2304,256]{1,0:T(8,128)} %get-tuple-element.4), kind=kLoop, calls=%fused_computation.31 | loop fusion | flops 589824 | bytes 4718592 | tf_op jit(solution)/shard_map/mul | solution.py:109
  289.2 0.9 broadcast_multiply_fusion.1
  (44 shorter events, 5.8 us)
Async XLA Ops:
  7.2 6.3 %copy-start.9 = (bf16[3,256,256]{2,1,0:T(8,128)(2,1)S(1)}, bf16[3,256,256]{2,1,0:T(8,128)(2,1)}, u32[]{:S(2)}) copy-start(bf16[3,256,256]{2,1,0:T(8,128)(2,1)} %param.7) | copy-start | bytes 1179652
  7.2 6.3 %copy-start = (bf16[1,17,2,64,256]{4,3,2,1,0:T(8,128)(2,1)S(1)}, bf16[1,17,2,64,256]{4,3,2,1,0:T(8,128)(2,1)}, u32[]{:S(2)}) copy-start(bf16[1,17,2,64,256]{4,3,2,1,0:T(8,128)(2,1)} %param.5) | copy-start | bytes 3342340
  7.2 113.7 %all-reduce.11.cloned.1.call-start = ((), (), s32[]{:S(2)}) async-start(), calls=%async_computation.1 | async-start | bytes 6291456 | tf_op jit(solution)/shard_map/psum | solution.py:104
  8.6 15.4 %collective-permute-start = (bf16[1,17,1,64,256]{4,3,2,1,0:T(8,128)(2,1)S(1)}, bf16[1,17,1,64,256]{4,3,2,1,0:T(8,128)(2,1)S(1)}, u32[]{:S(2)}, u32[]{:S(2)}) collective-permute-start(bf16[1,17,1,64,256]{4,3,2,1,0:T(8,128)(2,1)S(1)} %get-tuple-element.14), channel_id=1, source_target_pairs={{0,1},{1,2},{2,3},{3,4},{4,5},{5,6},{6,7},{7,8},{8,9},{9,10},{10,1... | collective-permute-start | bytes 1671176 | tf_op jit(solution)/shard_map/ppermute | solution.py:15
  12.2 16.0 %collective-permute-start.1 = (bf16[1,17,1,64,256]{4,3,2,1,0:T(8,128)(2,1)S(1)}, bf16[1,17,1,64,256]{4,3,2,1,0:T(8,128)(2,1)S(1)}, u32[]{:S(2)}, u32[]{:S(2)}) collective-permute-start(bf16[1,17,1,64,256]{4,3,2,1,0:T(8,128)(2,1)S(1)} %get-tuple-element.15), channel_id=1, source_target_pairs={{1,0},{2,1},{3,2},{4,3},{5,4},{6,5},{7,6},{8,7},{9,8},{10,9},{11,1... | collective-permute-start | bytes 1671176 | tf_op jit(solution)/shard_map/ppermute | solution.py:17
  14.2 14.0 %copy-start.1 = (bf16[1,17,2,64,256]{4,3,2,1,0:T(8,128)(2,1)S(1)}, bf16[1,17,2,64,256]{4,3,2,1,0:T(8,128)(2,1)}, u32[]{:S(2)}) copy-start(bf16[1,17,2,64,256]{4,3,2,1,0:T(8,128)(2,1)} %param.4) | copy-start | bytes 3342340
  31.7 1.3 copy-start.7
  35.8 6.0 %copy-start.3 = (bf16[2176,256]{1,0:T(8,128)(2,1)}, bf16[2176,256]{1,0:T(8,128)(2,1)S(1)}, u32[]{:S(2)}) copy-start(bf16[2176,256]{1,0:T(8,128)(2,1)S(1)} %get-tuple-element.16) | copy-start | bytes 3342340
  36.9 4.4 %copy-start.5 = (bf16[2176,256]{1,0:T(8,128)(2,1)}, bf16[2176,256]{1,0:T(8,128)(2,1)S(1)}, u32[]{:S(2)}) copy-start(bf16[2176,256]{1,0:T(8,128)(2,1)S(1)} %fusion.9) | copy-start | bytes 3342340
  42.1 1.0 copy-start.2
  44.2 241.7 %all-reduce.9.cloned.1.call-start = ((), (), s32[]{:S(2)}) async-start(), calls=%async_computation | async-start | bytes 6291456 | tf_op jit(solution)/shard_map/psum | solution.py:104
  46.6 8.1 %copy-start.4 = (bf16[2176,256]{1,0:T(8,128)(2,1)S(1)}, bf16[2176,256]{1,0:T(8,128)(2,1)}, u32[]{:S(2)}) copy-start(bf16[2176,256]{1,0:T(8,128)(2,1)} %copy-done.3) | copy-start | bytes 3342340
  49.1 76.8 %collective-permute-start.2 = (bf16[1,17,1,64,256]{4,3,2,1,0:T(8,128)(2,1)}, bf16[1,17,1,64,256]{4,3,2,1,0:T(8,128)(2,1)}, u32[]{:S(2)}, u32[]{:S(2)}) collective-permute-start(bf16[1,17,1,64,256]{4,3,2,1,0:T(8,128)(2,1)} %get-tuple-element.8), channel_id=1, source_target_pairs={{0,1},{1,2},{2,3},{3,4},{4,5},{5,6},{6,7},{7,8},{8,9},{9,10},{10,1... | collective-permute-start | bytes 1671176 | tf_op jit(solution)/shard_map/ppermute | solution.py:15
  53.4 72.5 %collective-permute-start.3 = (bf16[1,17,1,64,256]{4,3,2,1,0:T(8,128)(2,1)}, bf16[1,17,1,64,256]{4,3,2,1,0:T(8,128)(2,1)}, u32[]{:S(2)}, u32[]{:S(2)}) collective-permute-start(bf16[1,17,1,64,256]{4,3,2,1,0:T(8,128)(2,1)} %get-tuple-element.9), channel_id=1, source_target_pairs={{1,0},{2,1},{3,2},{4,3},{5,4},{6,5},{7,6},{8,7},{9,8},{10,9},{11,1... | collective-permute-start | bytes 1671176 | tf_op jit(solution)/shard_map/ppermute | solution.py:17
  123.4 2.5 copy-start.6
  130.7 1.3 copy-start.8
  285.8 3.4 %copy-start.10 = (f32[3,256,256]{2,1,0:T(8,128)S(1)}, f32[3,256,256]{2,1,0:T(8,128)}, u32[]{:S(2)}) copy-start(f32[3,256,256]{2,1,0:T(8,128)} %get-tuple-element.5) | copy-start | bytes 2359300
Sparse Core Ops, SparseCore 0:
  44.3 76.5 all-reduce.10
  124.5 161.2 all-reduce.8
